TPU v7x, 32 devices: a whole 2x2x4 slice. The times are simulated.
32 devices in a mesh: groups: 2 (over y), patch: 4 (over z), head: 4 (over x, core).
Axes of the slice: x: 2, y: 2, z: 4, core: 2. Of those that a mesh axis runs over, the one named last changes fastest.
Arguments:
- queries: bfloat16 [1536, 1536], P(('groups', 'patch'), 'head'), parts along dimension 0, may hold values from -12.5 to 12.5
- fresh_keys: bfloat16 [1536, 1536], P(('groups', 'patch'), 'head'), parts along dimension 0, may hold values from -5 to 5
- fresh_values: bfloat16 [1536, 1536], P(('groups', 'patch'), 'head'), parts along dimension 0, may hold values from -6 to 6
- stale_keys: bfloat16 [1536, 1536], P(('groups', 'patch'), 'head'), parts along dimension 0, may hold values from -5 to 5
- stale_values: bfloat16 [1536, 1536], P(('groups', 'patch'), 'head'), parts along dimension 0, may hold values from -6 to 6
- out_weight: bfloat16 [1536, 5120], P('head', 'patch'), may hold values from -0.21875 to 0.21875
- gate_scale: float32 [10240], P(('groups', 'head')), parts along dimension 0, may hold values from 1 to 4
Outputs:
- branch_out: float32 [1536, 5120], P(('groups', 'patch'), 'head'), parts along dimension 0
There are 2 independent parts, one for each index of `groups`. A program takes and returns all parts, laid end to end along the dimension named above; an argument that names none is the same for every part. Nothing has to cross between parts.
All inputs are finite; a program needn't handle non-finite values.
Results may differ from a plain program's by a relative error of at most 0.006.
Values may be sent and summed in bfloat16 or wider, within the bound.
No kernel may reach another device: no remote copies, remote signals or barrier semaphores. Data moves between devices by JAX's collectives and lax.ppermute only.
A program may use at most 64 MiB of HBM per device.

v0:
```python
import jax
import jax.numpy as jnp
from jax import lax
from jax.sharding import PartitionSpec as P

HEAD_DIM = 128
neg_large = -1e30


def head_view(matrix):
    return matrix.reshape(matrix.shape[0], -1, HEAD_DIM)


def block_scores(query_heads, key_block):
    return jnp.einsum(
        "qhd,khd->hqk", query_heads, head_view(key_block), preferred_element_type=jnp.float32
    ) * HEAD_DIM ** (-0.5)


def absorb(running, scores, value_block):
    run_max, run_total, run_acc = running
    new_max = jnp.maximum(run_max, jnp.max(scores, axis=2))
    factor = jnp.exp(run_max - new_max)
    weights = jnp.exp(scores - new_max[:, :, None])
    new_total = run_total * factor + jnp.sum(weights, axis=2)
    mixture = jnp.einsum(
        "hqk,khd->qhd",
        weights.astype(jnp.bfloat16),
        head_view(value_block),
        preferred_element_type=jnp.float32,
    )
    new_acc = run_acc * jnp.transpose(factor)[:, :, None] + mixture
    return (new_max, new_total, new_acc)


def empty_state(row_count, head_count):
    return (
        jnp.full((head_count, row_count), neg_large, jnp.float32),
        jnp.zeros((head_count, row_count), jnp.float32),
        jnp.zeros((row_count, head_count, HEAD_DIM), jnp.float32),
    )


def on_device(queries, fresh_keys, fresh_values, stale_keys, stale_values, out_weight, gate_scale):
    query_heads = head_view(queries)
    row_count = query_heads.shape[0]
    head_count = query_heads.shape[1]
    own_index = lax.axis_index("patch")
    own_start = own_index * row_count
    local = absorb(
        empty_state(row_count, head_count), block_scores(query_heads, fresh_keys), fresh_values
    )
    key_piece = lax.all_gather(stale_keys, "patch", axis=0, tiled=True)
    value_piece = lax.all_gather(stale_values, "patch", axis=0, tiled=True)
    key_count = key_piece.shape[0]
    key_step = 1024 if key_count > 1024 and key_count % 1024 == 0 else key_count

    def visit(block_index, inner):
        offset = block_index * key_step
        key_block = lax.dynamic_slice_in_dim(key_piece, offset, key_step, 0)
        value_block = lax.dynamic_slice_in_dim(value_piece, offset, key_step, 0)
        scores = block_scores(query_heads, key_block)
        position = offset + lax.iota(jnp.int32, key_step)
        own_rows = (position >= own_start) & (position < own_start + row_count)
        scores = jnp.where(own_rows[None, None, :], neg_large, scores)
        return absorb(inner, scores, value_block)

    run_max, run_total, run_acc = lax.fori_loop(0, key_count // key_step, visit, local)
    attended = (
        (run_acc / jnp.transpose(run_total)[:, :, None]).astype(jnp.bfloat16).reshape(row_count, -1)
    )
    partial_out = jnp.dot(
        attended,
        lax.all_gather(out_weight, "patch", axis=1, tiled=True),
        preferred_element_type=jnp.float32,
    )
    summed = lax.psum_scatter(partial_out, "head", scatter_dimension=1, tiled=True)
    return gate_scale[None, :] * summed


def solution(mesh):
    return jax.shard_map(
        on_device,
        mesh=mesh,
        in_specs=(
            P(("groups", "patch"), "head"),
            P(("groups", "patch"), "head"),
            P(("groups", "patch"), "head"),
            P(("groups", "patch"), "head"),
            P(("groups", "patch"), "head"),
            P("head", "patch"),
            P(("groups", "head")),
        ),
        out_specs=P(("groups", "patch"), "head"),
        check_vma=False,
    )
```

profile of v0, /device:TPU:0, one launch (start us, length us, event | category | flops | bytes accessed | tf_op | source)
XLA Modules:
  0.0 154.9 jit_solution(16892380855673942393)
XLA Ops:
  6.5 0.0 copy-start
  6.5 0.0 copy-start.2
  6.5 0.0 all-gather.2.cloned.1.call-start
  6.5 0.7 all-gather.2.cloned.1.call-update
  7.3 0.0 reduce-scatter.2.cloned.1.call-start
  7.3 0.0 copy-start.1
  7.3 20.8 %all_gather.9 = bf16[768,384]{1,0:T(8,128)(2,1)S(1)} all-gather(bf16[192,384]{1,0:T(8,128)(2,1)} %param.10), channel_id=1, replica_groups=mesh['groups'=2,'patch'=4,'head'=4] {'patch'}, dimensions={0}, use_global_device_ids=true | all-gather | bytes 737280 | tf_op jit(solution)/shard_map/all_gather | solution.py:53
  28.1 0.3 copy.27
  28.3 0.0 copy-done.2
  28.4 24.2 %all_gather.10 = bf16[768,384]{1,0:T(8,128)(2,1)S(1)} all-gather(bf16[192,384]{1,0:T(8,128)(2,1)S(1)} %copy-done.2), channel_id=1, replica_groups=mesh['groups'=2,'patch'=4,'head'=4] {'patch'}, dimensions={0}, use_global_device_ids=true | all-gather | bytes 737280 | tf_op jit(solution)/shard_map/all_gather | solution.py:54
  52.6 0.3 copy.30
  52.9 0.0 copy-done
  52.9 0.0 copy-done.1
  52.9 0.3 fusion.39
  53.2 0.5 fusion
  53.7 0.1 fusion.14
  53.8 0.5 fusion.1
  54.3 0.0 copy-start.4
  54.4 0.6 convolution_bitcast_fusion.1
  54.9 0.3 copy-done.4
  55.2 0.5 fusion.8
  55.7 43.2 %all-gather.2.cloned.1.call-done = bf16[384,5120]{1,0:T(8,128)(2,1)} async-done(((bf16[384,1280]{1,0:T(8,128)(2,1)}), bf16[384,5120]{1,0:T(8,128)(2,1)}) %all-gather.2.cloned.1.call-update) | async-done | bytes 3932176 | tf_op jit(solution)/shard_map/all_gather | solution.py:74
  98.9 5.2 %fusion.18 = f32[192,5120]{1,0:T(8,128)} fusion(bf16[384,5120]{1,0:T(8,128)(2,1)} %all-gather.2.cloned.1.call-done, bf16[3,24,8,128]{3,2,1,0:T(8,128)(2,1)S(1)} %fusion.8), kind=kOutput, calls=%fused_computation.23 | convolution fusion | flops 754974720 | bytes 8011776 | tf_op jit(solution)/shard_map/dot_general | solution.py:72
  104.1 0.0 copy-start.3
  104.1 0.0 reduce-scatter.2.cloned.1.call-update
  104.1 41.7 %reduce-scatter.2.cloned.1.call-done = f32[192,1280]{1,0:T(8,128)} async-done(((f32[192,5120]{1,0:T(8,128)}), f32[192,1280]{1,0:T(8,128)}) %reduce-scatter.2.cloned.1.call-update) | async-done | bytes 983056 | tf_op jit(solution)/shard_map/reduce_scatter | solution.py:77
  145.8 0.0 copy-done.3
  145.8 2.2 %broadcast_multiply_fusion = f32[192,1280]{1,0:T(8,128)} fusion(f32[192,1280]{1,0:T(8,128)} %reduce-scatter.2.cloned.1.call-done, f32[1280]{0:T(1024)S(1)} %copy-done.3), kind=kLoop, calls=%fused_computation.21 | loop fusion | flops 245760 | bytes 1971200 | tf_op jit(solution)/shard_map/mul | solution.py:78
  (3 shorter events, 0.0 us)
Async XLA Ops:
  6.5 46.3 %copy-start = (bf16[192,384]{1,0:T(8,128)(2,1)S(1)}, bf16[192,384]{1,0:T(8,128)(2,1)}, u32[]{:S(2)}) copy-start(bf16[192,384]{1,0:T(8,128)(2,1)} %param.7) | copy-start | bytes 442372
  6.5 21.8 %copy-start.2 = (bf16[192,384]{1,0:T(8,128)(2,1)S(1)}, bf16[192,384]{1,0:T(8,128)(2,1)}, u32[]{:S(2)}) copy-start(bf16[192,384]{1,0:T(8,128)(2,1)} %param.11) | copy-start | bytes 442372
  6.5 92.4 %all-gather.2.cloned.1.call-start = ((), (), s32[]{:S(2)}) async-start(), calls=%async_computation.1 | async-start | bytes 4915200 | tf_op jit(solution)/shard_map/all_gather | solution.py:74
  7.3 138.6 %reduce-scatter.2.cloned.1.call-start = ((), (), s32[]{:S(2)}) async-start(), calls=%async_computation.2 | async-start | bytes 4915200 | tf_op jit(solution)/shard_map/reduce_scatter | solution.py:77
  7.3 45.6 %copy-start.1 = (bf16[192,384]{1,0:T(8,128)(2,1)S(1)}, bf16[192,384]{1,0:T(8,128)(2,1)}, u32[]{:S(2)}) copy-start(bf16[192,384]{1,0:T(8,128)(2,1)} %param.8) | copy-start | bytes 442372
  54.3 0.9 copy-start.4
  104.1 41.8 %copy-start.3 = (f32[1280]{0:T(1024)S(1)}, f32[1280]{0:T(1024)}, u32[]{:S(2)}) copy-start(f32[1280]{0:T(1024)} %param.13) | copy-start | bytes 15364
Sparse Core Ops, SparseCore 0:
  8.9 89.9 all-gather.1
  104.2 41.5 reduce-scatter.1
where the time goes:
time: 155 us
  waiting for transfers between devices  85.7 us (55%)
  blocking collectives  45 us (29%)
  between operations  13.5 us (9%)
  matrix products  6.96 us (4%)
  other arithmetic  2.89 us (2%)
    all_gather x1, waiting for transfers between devices, on_device(): lax.all_gather(out_weight, 'patch', axis=1, tiled=True)  43.2 us
    reduce_scatter x1, waiting for transfers between devices, on_device(): lax.psum_scatter(partial_out, 'head', scatter_dimension=1, tiled=True)  41.7 us
    all_gather x1, blocking collectives, on_device(): value_piece = lax.all_gather(stale_values, 'patch', axis=0, tiled=True)  24.2 us
    all_gather x1, blocking collectives, on_device(): key_piece = lax.all_gather(stale_keys, 'patch', axis=0, tiled=True)  20.8 us
    dot_general x1, matrix products, on_device(): jnp.dot(attended, lax.all_gather(out_weight, 'patch', axis=1, tiled=True)...  5.18 us
  transfers between devices with their start and end apart: 2, of which 2 were waited for; matrix products, arithmetic and copies ran while one was open for 2% of the time, Pallas kernels for 0%

commit v1 on v0

--- a/solution.py
+++ b/solution.py
@@ -2,6 +2,7 @@
 import jax.numpy as jnp
 from jax import lax
 from jax.sharding import PartitionSpec as P
+from jax.lax import axis_index, ppermute, psum
 
 HEAD_DIM = 128
 neg_large = -1e30
@@ -51,7 +52,21 @@
         empty_state(row_count, head_count), block_scores(query_heads, fresh_keys), fresh_values
     )
     key_piece = lax.all_gather(stale_keys, "patch", axis=0, tiled=True)
-    value_piece = lax.all_gather(stale_values, "patch", axis=0, tiled=True)
+    back = psum(1, "patch")
+    by_rank = []
+    earlier, clean, outcome_arr = (back, axis_index("patch"), stale_values.shape[0])
+    for it in range(earlier):
+        by_rank.append((it, (it + 1) % earlier))
+    value_piece = jnp.zeros(
+        (*stale_values.shape[:0], earlier * outcome_arr, *stale_values.shape[1:]),
+        stale_values.dtype,
+    )
+    y1 = stale_values
+    for tick in range(earlier):
+        m_next = (clean - tick) % earlier
+        value_piece = lax.dynamic_update_slice_in_dim(value_piece, y1, m_next * outcome_arr, axis=0)
+        if tick < earlier - 1:
+            y1 = ppermute(y1, "patch", by_rank)
     key_count = key_piece.shape[0]
     key_step = 1024 if key_count > 1024 and key_count % 1024 == 0 else key_count
 

time: 155 us -> 158 us (1.019)
  blocking collectives: 45 us -> 23 us
  local copies, waits for them, and re-layouts: 0.84 us -> 14.1 us
  waiting for transfers between devices: 85.7 us -> 92.4 us
  starting transfers between devices: 0.04 us -> 4.4 us
    all_gather x1 -> x0, blocking collectives: 24.2 us -> none  [on_device(): value_piece = lax.all_gather(stale_values, 'patch', axis=0, tiled=True)]
    ppermute x0 -> x3, waiting for transfers between devices: none -> 20.7 us  [on_device(): y1 = ppermute(y1, 'patch', by_rank)]
    all_gather x1, waiting for transfers between devices: 43.2 us -> 28.2 us  [on_device(): lax.all_gather(out_weight, 'patch', axis=1, tiled=True)]
    dynamic_update_slice x0 -> x4, local copies, waits for them, and re-layouts: none -> 12.7 us  [on_device(): lax.dynamic_update_slice_in_dim(value_piece, y1, m_next * outcome_arr, ax...]
    ppermute x0 -> x3, starting transfers between devices: none -> 4.36 us  [on_device(): y1 = ppermute(y1, 'patch', by_rank)]
    all_gather x1, blocking collectives: 20.8 us -> 23 us  [on_device(): key_piece = lax.all_gather(stale_keys, 'patch', axis=0, tiled=True)]
  transfers between devices with their start and end apart: 2 -> 5, of which waited for: 2 -> 4; matrix products, arithmetic and copies ran while one was open for 2% -> 10% of each run, Pallas kernels for 0% -> 0%
where the time goes in v1:
time: 158 us; the launch traced here: 157 us
  waiting for transfers between devices  92.4 us (58%)
  blocking collectives  23 us (15%)
  local copies, waits for them, and re-layouts  14.1 us (9%)
  between operations  13.6 us (9%)
  matrix products  6.97 us (4%)
  starting transfers between devices  4.4 us (3%)
  other arithmetic  2.88 us (2%)
    reduce_scatter x1, waiting for transfers between devices, on_device(): lax.psum_scatter(partial_out, 'head', scatter_dimension=1, tiled=True)  42.8 us
    all_gather x1, waiting for transfers between devices, on_device(): lax.all_gather(out_weight, 'patch', axis=1, tiled=True)  28.2 us
    all_gather x1, blocking collectives, on_device(): key_piece = lax.all_gather(stale_keys, 'patch', axis=0, tiled=True)  23 us
    ppermute x3, waiting for transfers between devices, on_device(): y1 = ppermute(y1, 'patch', by_rank)  20.7 us
    dynamic_update_slice x4, local copies, waits for them, and re-layouts, on_device(): lax.dynamic_update_slice_in_dim(value_piece, y1, m_next * outcome_arr, ax...  12.7 us
    dot_general x1, matrix products, on_device(): jnp.dot(attended, lax.all_gather(out_weight, 'patch', axis=1, tiled=True)...  5.21 us
    ppermute x3, starting transfers between devices, on_device(): y1 = ppermute(y1, 'patch', by_rank)  4.36 us
  transfers between devices with their start and end apart: 5, of which 4 were waited for; matrix products, arithmetic and copies ran while one was open for 10% of the time, Pallas kernels for 0%

profile of v1, /device:TPU:0, one launch (start us, length us, event | category | flops | bytes accessed | tf_op | source)
XLA Modules:
  0.0 157.3 jit_solution(10245016405331228371)
XLA Ops:
  6.5 0.0 copy-start
  6.5 0.0 copy-start.1
  6.5 0.0 all-gather.2.cloned.1.call-start
  6.5 0.7 all-gather.2.cloned.1.call-update
  7.3 0.0 reduce-scatter.2.cloned.1.call-start
  7.3 1.0 copy.31
  8.4 3.1 %collective-permute-start = (bf16[192,384]{0,1:T(8,128)(2,1)S(1)}, bf16[192,384]{0,1:T(8,128)(2,1)}, u32[]{:S(2)}, u32[]{:S(2)}) collective-permute-start(bf16[192,384]{0,1:T(8,128)(2,1)S(1)} %copy.31), channel_id=1, source_target_pairs={{0,4},{4,8},{8,12},{12,0},{1,5},{5,9},{9,13},{13,1},{2,6},{6,10},{... | collective-permute-start | bytes 442376 | tf_op jit(solution)/shard_map/ppermute | solution.py:69
  11.5 23.0 %all_gather.6 = bf16[768,384]{1,0:T(8,128)(2,1)S(1)} all-gather(bf16[192,384]{1,0:T(8,128)(2,1)} %param.10), channel_id=1, replica_groups=mesh['groups'=2,'patch'=4,'head'=4] {'patch'}, dimensions={0}, use_global_device_ids=true | all-gather | bytes 737280 | tf_op jit(solution)/shard_map/all_gather | solution.py:54
  34.5 0.3 copy.28
  34.7 0.0 copy-done
  34.7 0.0 copy-done.1
  34.8 0.3 fusion.39
  35.0 0.5 fusion
  35.5 0.0 copy-start.2
  35.5 0.5 fusion.1
  36.2 2.6 %dynamic_update_slice.12 = bf16[768,384]{0,1:T(8,128)(2,1)S(1)} dynamic-update-slice(bf16[768,384]{0,1:T(8,128)(2,1)S(1)} %broadcast_in_dim.43, bf16[192,384]{0,1:T(8,128)(2,1)S(1)} %copy.31, s32[]{:T(128)S(6)} %select_n.41, s32[]{:T(128)} %constant.67.clone.1) | dynamic-update-slice | bytes 294916 | tf_op jit(solution)/shard_map/dynamic_update_slice | solution.py:67
  38.8 0.1 fusion.14
  38.9 0.0 collective-permute-done
  38.9 0.8 collective-permute-start.1
  39.8 12.3 %collective-permute-done.1 = bf16[192,384]{0,1:T(8,128)(2,1)} collective-permute-done((bf16[192,384]{0,1:T(8,128)(2,1)}, bf16[192,384]{0,1:T(8,128)(2,1)}, u32[]{:S(2)}, u32[]{:S(2)}) %collective-permute-start.1) | collective-permute-done | bytes 147488 | tf_op jit(solution)/shard_map/ppermute | solution.py:69
  52.1 0.4 collective-permute-start.2
  52.5 0.0 copy-done.2
  52.5 0.4 fusion.4
  52.9 3.4 %dynamic_update_slice.13 = bf16[768,384]{0,1:T(8,128)(2,1)S(1)} dynamic-update-slice(bf16[768,384]{0,1:T(8,128)(2,1)S(1)} %dynamic_update_slice.12, bf16[192,384]{0,1:T(8,128)(2,1)} %collective-permute-done, s32[]{:T(128)S(6)} %select_n.43, s32[]{:T(128)} %constant.67.clone.1) | dynamic-update-slice | bytes 294916 | tf_op jit(solution)/shard_map/dynamic_update_slice | solution.py:67
  56.4 3.0 %dynamic_update_slice.14 = bf16[768,384]{0,1:T(8,128)(2,1)S(1)} dynamic-update-slice(bf16[768,384]{0,1:T(8,128)(2,1)S(1)} %dynamic_update_slice.13, bf16[192,384]{0,1:T(8,128)(2,1)} %collective-permute-done.1, s32[]{:T(128)S(6)} %select_n.45, s32[]{:T(128)} %constant.67.clone.1) | dynamic-update-slice | bytes 294916 | tf_op jit(solution)/shard_map/dynamic_update_slice | solution.py:67
  59.4 8.3 %collective-permute-done.2 = bf16[192,384]{0,1:T(8,128)(2,1)} collective-permute-done((bf16[192,384]{0,1:T(8,128)(2,1)}, bf16[192,384]{0,1:T(8,128)(2,1)}, u32[]{:S(2)}, u32[]{:S(2)}) %collective-permute-start.2) | collective-permute-done | bytes 147488 | tf_op jit(solution)/shard_map/ppermute | solution.py:69
  67.7 3.7 %dynamic_update_slice.15 = bf16[768,384]{0,1:T(8,128)(2,1)S(1)} dynamic-update-slice(bf16[768,384]{0,1:T(8,128)(2,1)S(1)} %dynamic_update_slice.14, bf16[192,384]{0,1:T(8,128)(2,1)} %collective-permute-done.2, s32[]{:T(128)S(6)} %select_n.47, s32[]{:T(128)} %constant.67.clone.1) | dynamic-update-slice | bytes 294916 | tf_op jit(solution)/shard_map/dynamic_update_slice | solution.py:67
  71.4 0.6 fusion.8
  72.0 28.2 %all-gather.2.cloned.1.call-done = bf16[384,5120]{1,0:T(8,128)(2,1)} async-done(((bf16[384,1280]{1,0:T(8,128)(2,1)}), bf16[384,5120]{1,0:T(8,128)(2,1)}) %all-gather.2.cloned.1.call-update) | async-done | bytes 3932176 | tf_op jit(solution)/shard_map/all_gather | solution.py:89
  100.2 5.2 %fusion.18 = f32[192,5120]{1,0:T(8,128)} fusion(bf16[384,5120]{1,0:T(8,128)(2,1)} %all-gather.2.cloned.1.call-done, bf16[3,24,8,128]{3,2,1,0:T(8,128)(2,1)S(1)} %fusion.8), kind=kOutput, calls=%fused_computation.23 | convolution fusion | flops 754974720 | bytes 8011776 | tf_op jit(solution)/shard_map/dot_general | solution.py:87
  105.4 0.0 copy-start.3
  105.4 0.0 reduce-scatter.2.cloned.1.call-update
  105.4 42.8 %reduce-scatter.2.cloned.1.call-done = f32[192,1280]{1,0:T(8,128)} async-done(((f32[192,5120]{1,0:T(8,128)}), f32[192,1280]{1,0:T(8,128)}) %reduce-scatter.2.cloned.1.call-update) | async-done | bytes 983056 | tf_op jit(solution)/shard_map/reduce_scatter | solution.py:92
  148.2 0.0 copy-done.3
  148.2 2.2 %broadcast_multiply_fusion = f32[192,1280]{1,0:T(8,128)} fusion(f32[192,1280]{1,0:T(8,128)} %reduce-scatter.2.cloned.1.call-done, f32[1280]{0:T(1024)S(1)} %copy-done.3), kind=kLoop, calls=%fused_computation.21 | loop fusion | flops 245760 | bytes 1971200 | tf_op jit(solution)/shard_map/mul | solution.py:93
  (4 shorter events, 0.1 us)
Async XLA Ops:
  6.5 28.2 %copy-start = (bf16[192,384]{1,0:T(8,128)(2,1)S(1)}, bf16[192,384]{1,0:T(8,128)(2,1)}, u32[]{:S(2)}) copy-start(bf16[192,384]{1,0:T(8,128)(2,1)} %param.7) | copy-start | bytes 442372
  6.5 28.2 %copy-start.1 = (bf16[192,384]{1,0:T(8,128)(2,1)S(1)}, bf16[192,384]{1,0:T(8,128)(2,1)}, u32[]{:S(2)}) copy-start(bf16[192,384]{1,0:T(8,128)(2,1)} %param.8) | copy-start | bytes 442372
  6.5 93.7 %all-gather.2.cloned.1.call-start = ((), (), s32[]{:S(2)}) async-start(), calls=%async_computation.1 | async-start | bytes 4915200 | tf_op jit(solution)/shard_map/all_gather | solution.py:89
  7.3 141.0 %reduce-scatter.2.cloned.1.call-start = ((), (), s32[]{:S(2)}) async-start(), calls=%async_computation.2 | async-start | bytes 4915200 | tf_op jit(solution)/shard_map/reduce_scatter | solution.py:92
  8.4 30.6 %collective-permute-start = (bf16[192,384]{0,1:T(8,128)(2,1)S(1)}, bf16[192,384]{0,1:T(8,128)(2,1)}, u32[]{:S(2)}, u32[]{:S(2)}) collective-permute-start(bf16[192,384]{0,1:T(8,128)(2,1)S(1)} %copy.31), channel_id=1, source_target_pairs={{0,4},{4,8},{8,12},{12,0},{1,5},{5,9},{9,13},{13,1},{2,6},{6,10},{... | collective-permute-start | bytes 442376 | tf_op jit(solution)/shard_map/ppermute | solution.py:69
  35.5 17.0 %copy-start.2 = (bf16[192,384]{1,0:T(8,128)(2,1)S(1)}, bf16[192,384]{1,0:T(8,128)(2,1)}, u32[]{:S(2)}) copy-start(bf16[192,384]{1,0:T(8,128)(2,1)} %param.9) | copy-start | bytes 442372
  38.9 13.2 %collective-permute-start.1 = (bf16[192,384]{0,1:T(8,128)(2,1)}, bf16[192,384]{0,1:T(8,128)(2,1)}, u32[]{:S(2)}, u32[]{:S(2)}) collective-permute-start(bf16[192,384]{0,1:T(8,128)(2,1)} %collective-permute-done), channel_id=1, source_target_pairs={{0,4},{4,8},{8,12},{12,0},{1,5},{5,9},{9,13},{13,1},{2,6},{6,10},{... | collective-permute-start | bytes 442376 | tf_op jit(solution)/shard_map/ppermute | solution.py:69
  52.1 15.6 %collective-permute-start.2 = (bf16[192,384]{0,1:T(8,128)(2,1)}, bf16[192,384]{0,1:T(8,128)(2,1)}, u32[]{:S(2)}, u32[]{:S(2)}) collective-permute-start(bf16[192,384]{0,1:T(8,128)(2,1)} %collective-permute-done.1), channel_id=1, source_target_pairs={{0,4},{4,8},{8,12},{12,0},{1,5},{5,9},{9,13},{13,1},{2,6},{6,10},{... | collective-permute-start | bytes 442376 | tf_op jit(solution)/shard_map/ppermute | solution.py:69
  105.4 42.8 %copy-start.3 = (f32[1280]{0:T(1024)S(1)}, f32[1280]{0:T(1024)}, u32[]{:S(2)}) copy-start(f32[1280]{0:T(1024)} %param.13) | copy-start | bytes 15364
Sparse Core Ops, SparseCore 0:
  8.9 91.2 all-gather.1
  105.6 42.6 reduce-scatter.1
